TPU v7x, 32 devices: a whole 2x2x4 slice. The times are simulated.
32 devices in a mesh: dp: 8 (over z, x), tensor: 4 (over y, core).
Axes of the slice: x: 2, y: 2, z: 4, core: 2. Of those that a mesh axis runs over, the one named last changes fastest.
Arguments:
- images: bfloat16 [16, 197, 768], P('dp'), may hold values from -6 to 6
- image_counts: int32 [8], P('dp'), may hold values from 1 to 2, as said below
- first_norm_gain: float32 [768], replicated, may hold values from 0.5 to 1.5
- first_norm_bias: float32 [768], replicated, may hold values from -3 to 3
- qkv_weight: bfloat16 [768, 3, 768], P(None, None, 'tensor'), may hold values from -2 to 2
- qv_bias: float32 [2, 768], P(None, 'tensor'), may hold values from -3 to 3
- out_weight: bfloat16 [768, 768], P('tensor'), may hold values from -1.25 to 1.25
- out_bias: float32 [768], replicated, may hold values from -3 to 3
- second_norm_gain: float32 [768], replicated, may hold values from 0.5 to 1.5
- second_norm_bias: float32 [768], replicated, may hold values from -3 to 3
- fc1_weight: bfloat16 [768, 3072], P(None, 'tensor'), may hold values from -0.21875 to 0.21875
- fc1_bias: float32 [3072], P('tensor'), may hold values from -3 to 3
- fc2_weight: bfloat16 [3072, 768], P('tensor'), may hold values from -0.15625 to 0.15625
- fc2_bias: float32 [768], replicated, may hold values from -3 to 3
- cotangent: bfloat16 [16, 197, 768], P('dp'), may hold values from -6 to 6
Outputs:
- block_out: bfloat16 [16, 197, 768], P('dp')
- input_grad: bfloat16 [16, 197, 768], P('dp')
- grad_first_norm_gain: float32 [768], replicated
- grad_first_norm_bias: float32 [768], replicated
- grad_qkv_weight: float32 [768, 3, 768], P(None, None, 'tensor')
- grad_qv_bias: float32 [2, 768], P(None, 'tensor')
- grad_out_weight: float32 [768, 768], P('tensor')
- grad_out_bias: float32 [768], replicated
- grad_second_norm_gain: float32 [768], replicated
- grad_second_norm_bias: float32 [768], replicated
- grad_fc1_weight: float32 [768, 3072], P(None, 'tensor')
- grad_fc1_bias: float32 [3072], P('tensor')
- grad_fc2_weight: float32 [3072, 768], P('tensor')
- grad_fc2_bias: float32 [768], replicated
Inputs may be any that keep to these rules, and one draw needn't show every extreme that they name: `image_counts`: some index of dp has 2 live slots and some has 1; live slots come first in each index's block of 2.
All inputs are finite; a program needn't handle non-finite values.
Results may differ from a plain program's by a relative error of at most 0.02.
Values may be sent and summed in bfloat16 or wider, within the bound.
A program may use at most 128 MiB of HBM per device.

v0:
```python
import jax
import jax.numpy as jnp
from jax import lax
from jax.sharding import PartitionSpec as P

HEAD_DIM = 64
EPS = 1e-06
ROOT_HALF = 0.7071067811865476
INV_ROOT_TAU = 0.3989422804014327


def to_half(array_in):
    return array_in.astype(jnp.bfloat16)


def norm_forward(row_values, gain_vec, shift_vec):
    centre = row_values - jnp.mean(row_values, axis=-1, keepdims=True)
    inverse = lax.rsqrt(jnp.mean(centre * centre, axis=-1, keepdims=True) + EPS)
    scaled = centre * inverse
    return (scaled * gain_vec + shift_vec, scaled, inverse)


def norm_backward(grad_out, scaled, inverse, gain_vec):
    grad_scaled = grad_out * gain_vec
    grad_rows = inverse * (
        grad_scaled
        - jnp.mean(grad_scaled, axis=-1, keepdims=True)
        - scaled * jnp.mean(grad_scaled * scaled, axis=-1, keepdims=True)
    )
    return (grad_rows, jnp.sum(grad_out * scaled, axis=0), jnp.sum(grad_out, axis=0))


def gelu_value(pre_act):
    return 0.5 * pre_act * (1.0 + jax.scipy.special.erf(pre_act * ROOT_HALF))


def gelu_slope(pre_act):
    return (
        0.5 * (1.0 + jax.scipy.special.erf(pre_act * ROOT_HALF))
        + pre_act * jnp.exp(-0.5 * pre_act * pre_act) * INV_ROOT_TAU
    )


def per_device(
    images,
    image_counts,
    first_norm_gain,
    first_norm_bias,
    qkv_weight,
    qv_bias,
    out_weight,
    out_bias,
    second_norm_gain,
    second_norm_bias,
    fc1_weight,
    fc1_bias,
    fc2_weight,
    fc2_bias,
    cotangent,
):
    f32 = jnp.float32
    slot_count, length, model_width = images.shape
    local_width = qkv_weight.shape[2]
    local_heads = local_width // HEAD_DIM
    row_count = slot_count * length
    score_scale = HEAD_DIM ** (-0.5)
    live_slots = (jnp.arange(slot_count, dtype=jnp.int32) < image_counts[0]).astype(f32)
    row_live = jnp.broadcast_to(live_slots[:, None], (slot_count, length)).reshape(row_count, 1)
    head_shape = (slot_count, length, local_heads, HEAD_DIM)
    row_values = images.reshape(row_count, model_width).astype(f32)
    norm_one, scaled_one, inverse_one = norm_forward(row_values, first_norm_gain, first_norm_bias)
    norm_one = to_half(norm_one)
    qkv_flat = qkv_weight.reshape(model_width, 3 * local_width)
    qkv_shift = jnp.stack([qv_bias[0], jnp.zeros_like(qv_bias[0]), qv_bias[1]])
    qkv_rows = to_half(
        jnp.dot(norm_one, qkv_flat, preferred_element_type=f32).reshape(row_count, 3, local_width)
        + qkv_shift
    )
    queries = qkv_rows[:, 0].reshape(head_shape)
    key_heads = qkv_rows[:, 1].reshape(head_shape)
    value_heads = qkv_rows[:, 2].reshape(head_shape)
    scores = (
        jnp.einsum("bqhd,bkhd->bhqk", queries, key_heads, preferred_element_type=f32) * score_scale
    )
    row_peak = jnp.max(scores, axis=-1, keepdims=True)
    log_total = row_peak + jnp.log(jnp.sum(jnp.exp(scores - row_peak), axis=-1, keepdims=True))
    probs_full = jnp.exp(scores - log_total)
    probs_half = to_half(probs_full)
    context = to_half(
        jnp.einsum("bhqk,bkhd->bqhd", probs_half, value_heads, preferred_element_type=f32)
    )
    context_rows = context.reshape(row_count, local_width)
    attn_part = jnp.dot(context_rows, out_weight, preferred_element_type=f32)
    resid_rows = (
        row_values
        + lax.psum(attn_part.astype(jnp.bfloat16), "tensor").astype(jnp.float32)
        + out_bias
    )
    norm_two, scaled_two, inverse_two = norm_forward(resid_rows, second_norm_gain, second_norm_bias)
    norm_two = to_half(norm_two)
    pre_act = jnp.dot(norm_two, fc1_weight, preferred_element_type=f32) + fc1_bias
    act_half = to_half(gelu_value(pre_act))
    mlp_part = jnp.dot(act_half, fc2_weight, preferred_element_type=f32)
    final_rows = (
        resid_rows
        + lax.psum(mlp_part.astype(jnp.bfloat16), "tensor").astype(jnp.float32)
        + fc2_bias
    )
    block_out = to_half(final_rows * row_live).reshape(slot_count, length, model_width)
    inv_images = 1.0 / (slot_count * lax.axis_size("dp"))
    grad_final = cotangent.reshape(row_count, model_width).astype(f32) * row_live
    grad_final_half = to_half(grad_final)
    grad_act = jnp.dot(grad_final_half, fc2_weight.T, preferred_element_type=f32)
    grad_pre = grad_act * gelu_slope(pre_act)
    grad_pre_half = to_half(grad_pre)
    two_part = jnp.dot(grad_pre_half, fc1_weight.T, preferred_element_type=f32)
    grad_norm_two = lax.psum(two_part.astype(jnp.bfloat16), "tensor").astype(jnp.float32)
    back_two, gain_two, shift_two = norm_backward(
        grad_norm_two, scaled_two, inverse_two, second_norm_gain
    )
    mlp_grads = (
        jnp.dot(norm_two.T, grad_pre_half, preferred_element_type=f32) * inv_images,
        jnp.sum(grad_pre, axis=0, keepdims=True) * inv_images,
        jnp.dot(act_half.T, grad_final_half, preferred_element_type=f32) * inv_images,
        jnp.stack([gain_two, shift_two, jnp.sum(grad_final, axis=0)]) * inv_images,
    )
    grad_resid = grad_final + back_two
    grad_resid_half = to_half(grad_resid)
    grad_context = to_half(
        jnp.dot(grad_resid_half, out_weight.T, preferred_element_type=f32)
    ).reshape(head_shape)
    grad_probs = jnp.einsum(
        "bqhd,bkhd->bhqk", grad_context, value_heads, preferred_element_type=f32
    )
    grad_scores = to_half(
        probs_full
        * (grad_probs - jnp.sum(probs_full * grad_probs, axis=-1, keepdims=True))
        * score_scale
    )
    grad_queries = jnp.einsum(
        "bhqk,bkhd->bqhd", grad_scores, key_heads, preferred_element_type=f32
    ).reshape(row_count, local_width)
    grad_keys = jnp.einsum(
        "bhqk,bqhd->bkhd", grad_scores, queries, preferred_element_type=f32
    ).reshape(row_count, local_width)
    grad_values = jnp.einsum(
        "bhqk,bqhd->bkhd", probs_half, grad_context, preferred_element_type=f32
    ).reshape(row_count, local_width)
    grad_qkv_half = to_half(jnp.stack([grad_queries, grad_keys, grad_values], axis=1)).reshape(
        row_count, 3 * local_width
    )
    one_part = jnp.dot(grad_qkv_half, qkv_flat.T, preferred_element_type=f32)
    grad_norm_one = lax.psum(one_part.astype(jnp.bfloat16), "tensor").astype(jnp.float32)
    back_one, gain_one, shift_one = norm_backward(
        grad_norm_one, scaled_one, inverse_one, first_norm_gain
    )
    input_grad = to_half(grad_resid + back_one).reshape(slot_count, length, model_width)
    attn_grads = (
        jnp.dot(norm_one.T, grad_qkv_half, preferred_element_type=f32) * inv_images,
        jnp.stack([jnp.sum(grad_queries, axis=0), jnp.sum(grad_values, axis=0)]) * inv_images,
        jnp.dot(context_rows.T, grad_resid_half, preferred_element_type=f32) * inv_images,
        jnp.stack([gain_one, shift_one, jnp.sum(grad_resid, axis=0)]) * inv_images,
    )
    shares = (
        lax.psum_scatter(attn_grads[0], "dp", scatter_dimension=1, tiled=True),
        lax.psum_scatter(attn_grads[1], "dp", scatter_dimension=1, tiled=True),
        lax.psum_scatter(attn_grads[2], "dp", scatter_dimension=1, tiled=True),
        lax.psum_scatter(attn_grads[3], "dp", scatter_dimension=1, tiled=True),
        lax.psum_scatter(mlp_grads[0], "dp", scatter_dimension=1, tiled=True),
        lax.psum_scatter(mlp_grads[1], "dp", scatter_dimension=1, tiled=True),
        lax.psum_scatter(mlp_grads[2], "dp", scatter_dimension=1, tiled=True),
        lax.psum_scatter(mlp_grads[3], "dp", scatter_dimension=1, tiled=True),
    )
    gathered = (
        lax.all_gather(shares[0].astype(jnp.bfloat16), "dp", axis=1, tiled=True).astype(
            jnp.float32
        ),
        lax.all_gather(shares[1].astype(jnp.bfloat16), "dp", axis=1, tiled=True).astype(
            jnp.float32
        ),
        lax.all_gather(shares[2].astype(jnp.bfloat16), "dp", axis=1, tiled=True).astype(
            jnp.float32
        ),
        lax.all_gather(shares[3].astype(jnp.bfloat16), "dp", axis=1, tiled=True).astype(
            jnp.float32
        ),
        lax.all_gather(shares[4].astype(jnp.bfloat16), "dp", axis=1, tiled=True).astype(
            jnp.float32
        ),
        lax.all_gather(shares[5].astype(jnp.bfloat16), "dp", axis=1, tiled=True).astype(
            jnp.float32
        ),
        lax.all_gather(shares[6].astype(jnp.bfloat16), "dp", axis=1, tiled=True).astype(
            jnp.float32
        ),
        lax.all_gather(shares[7].astype(jnp.bfloat16), "dp", axis=1, tiled=True).astype(
            jnp.float32
        ),
    )
    attn_full = gathered[:4]
    mlp_full = gathered[4:]
    return (
        block_out,
        input_grad,
        attn_full[3][0],
        attn_full[3][1],
        attn_full[0].reshape(model_width, 3, local_width),
        attn_full[1],
        attn_full[2],
        attn_full[3][2],
        mlp_full[3][0],
        mlp_full[3][1],
        mlp_full[0],
        mlp_full[1][0],
        mlp_full[2],
        mlp_full[3][2],
    )


def solution(mesh):
    placed = (
        P("dp", None, None),
        P("dp"),
        P(),
        P(),
        P(None, None, "tensor"),
        P(None, "tensor"),
        P("tensor", None),
        P(),
        P(),
        P(),
        P(None, "tensor"),
        P("tensor"),
        P("tensor", None),
        P(),
        P("dp", None, None),
    )
    return jax.shard_map(
        per_device,
        mesh=mesh,
        in_specs=placed,
        out_specs=(
            P("dp", None, None),
            P("dp", None, None),
            P(),
            P(),
            P(None, None, "tensor"),
            P(None, "tensor"),
            P("tensor", None),
            P(),
            P(),
            P(),
            P(None, "tensor"),
            P("tensor"),
            P("tensor", None),
            P(),
        ),
        check_vma=False,
    )
```

profile of v0, /device:TPU:0, one launch (start us, length us, event | category | flops | bytes accessed | tf_op | source)
XLA Modules:
  0.0 741.2 jit_solution(13153335465204012786)
XLA Ops:
  25.3 33.3 %all-reduce.7.cloned.1.call-done = bf16[394,768]{1,0:T(8,128)(2,1)} async-done(((bf16[394,768]{1,0:T(8,128)(2,1)}), bf16[394,768]{1,0:T(8,128)(2,1)}) %all-reduce.7.cloned.1.call-update) | async-done | bytes 605200 | tf_op jit(solution)/shard_map/psum | solution.py:96
  69.7 31.1 %all-reduce.9.cloned.1.call-done = bf16[394,768]{1,0:T(8,128)(2,1)} async-done(((bf16[394,768]{1,0:T(8,128)(2,1)}), bf16[394,768]{1,0:T(8,128)(2,1)}) %all-reduce.9.cloned.1.call-update) | async-done | bytes 605200 | tf_op jit(solution)/shard_map/psum | solution.py:117
  107.8 4.5 fusion.69
  112.3 3.8 fusion.34
  130.3 3.4 convolution_multiply_fusion.1
  137.3 3.6 convolution_multiply_fusion
  142.0 26.2 %all-reduce.11.cloned.1.call-done = (bf16[394,768]{1,0:T(8,128)(2,1)}, bf16[394,768]{1,0:T(8,128)(2,1)}) async-done(((bf16[394,768]{1,0:T(8,128)(2,1)}, bf16[394,768]{1,0:T(8,128)(2,1)}), (bf16[394,768]{1,0:T(8,128)(2,1)}, bf16[394,768]{1,0:T(8,128)(2,1)})) %all-reduce.11.cloned.1.call-update) | async-done | bytes 1210384 | tf_op jit(solution)/shard_map/psum | solution.py:106
  177.2 3.1 convolution_multiply_fusion.2
  180.4 61.4 %reduce-scatter.19.cloned.1.call-done = f32[768,96]{0,1:T(8,128)} async-done(((f32[768,768]{0,1:T(8,128)}), f32[768,96]{0,1:T(8,128)}) %reduce-scatter.19.cloned.1.call-update) | async-done | bytes 294928 | tf_op jit(solution)/shard_map/reduce_scatter | solution.py:169
  245.3 60.9 %reduce-scatter.29.cloned.1.call-done = f32[96,1]{1,0:T(8,128)} async-done(((f32[768,1]{1,0:T(8,128)}), f32[96,1]{1,0:T(8,128)}) %reduce-scatter.29.cloned.1.call-update) | async-done | bytes 400
  307.3 19.5 %all-reduce = bf16[768]{0:T(1024)(128)(2,1)S(1)} all-reduce(bf16[768]{0:T(1024)(128)(2,1)S(1)} %dynamic-update-slice), channel_id=1, replica_groups=mesh['dp'=8,'tensor'=4] {'dp'}, use_global_device_ids=true, to_apply=%add | all-reduce | flops 768 | bytes 3072
  327.6 17.2 %all-reduce.1 = bf16[2,192]{1,0:T(2,128)(2,1)S(1)} all-reduce(f32[2,192]{1,0:T(2,128)S(1)} %maximum_multiply_fusion.2), channel_id=4, replica_groups=mesh['dp'=8,'tensor'=4] {'dp'}, use_global_device_ids=true, to_apply=%region_22.0.clone | all-reduce | flops 384 | bytes 2304
  344.8 18.3 %all-gather.1 = bf16[8,24,2]{1,2,0:T(2,128)(2,1)S(1)} all-gather(bf16[1,24,2]{1,2,0:T(2,128)(2,1)S(1)} %fusion.60), channel_id=1, replica_groups=mesh['dp'=8,'tensor'=4] {'dp'}, dimensions={0}, use_global_device_ids=true | all-gather | bytes 864 | tf_op jit(solution)/shard_map/all_gather | solution.py:178
  363.8 7.4 %reduce-scatter.27.cloned.1.call-done = f32[96,3]{1,0:T(8,128)} async-done(((f32[768,3]{1,0:T(8,128)}), f32[96,3]{1,0:T(8,128)}) %reduce-scatter.27.cloned.1.call-update) | async-done | bytes 1168
  372.1 19.0 %all-gather.2 = bf16[8,96,3]{1,2,0:T(4,128)(2,1)S(1)} all-gather(bf16[1,96,3]{1,2,0:T(4,128)(2,1)S(1)} %bitcast.107), channel_id=1, replica_groups=mesh['dp'=8,'tensor'=4] {'dp'}, dimensions={0}, use_global_device_ids=true | all-gather | bytes 5184 | tf_op jit(solution)/shard_map/all_gather | solution.py:196
  391.1 52.8 %reduce-scatter.21.cloned.1.call-done = f32[768,96]{0,1:T(8,128)} async-done(((f32[768,768]{0,1:T(8,128)}), f32[768,96]{0,1:T(8,128)}) %reduce-scatter.21.cloned.1.call-update) | async-done | bytes 294928 | tf_op jit(solution)/shard_map/reduce_scatter | solution.py:171
  456.9 51.7 %reduce-scatter.23.cloned.1.call-done = f32[96,3]{1,0:T(8,128)} async-done(((f32[768,3]{1,0:T(8,128)}), f32[96,3]{1,0:T(8,128)}) %reduce-scatter.23.cloned.1.call-update) | async-done | bytes 1168
  509.4 18.7 %all-gather = bf16[8,96,3]{1,2,0:T(4,128)(2,1)S(1)} all-gather(bf16[1,96,3]{1,2,0:T(4,128)(2,1)S(1)} %bitcast.108), channel_id=1, replica_groups=mesh['dp'=8,'tensor'=4] {'dp'}, dimensions={0}, use_global_device_ids=true | all-gather | bytes 5184 | tf_op jit(solution)/shard_map/all_gather | solution.py:184
  528.8 45.3 %reduce-scatter.25.cloned.1.call-done = f32[96,192]{1,0:T(8,128)} async-done(((f32[768,192]{1,0:T(8,128)}), f32[96,192]{1,0:T(8,128)}) %reduce-scatter.25.cloned.1.call-update) | async-done | bytes 73744
  575.2 31.8 %all_gather.27 = bf16[192,768]{0,1:T(8,128)(2,1)S(1)} all-gather(bf16[192,96]{0,1:T(8,128)(2,1)S(1)} %copy.157), channel_id=1, replica_groups=mesh['dp'=8,'tensor'=4] {'dp'}, dimensions={1}, use_global_device_ids=true | all-gather | bytes 331776 | tf_op jit(solution)/shard_map/all_gather | solution.py:181
  608.0 36.5 %reduce-scatter.17.cloned.1.call-done = f32[768,72]{0,1:T(8,128)} async-done(((f32[768,576]{0,1:T(8,128)}), f32[768,72]{0,1:T(8,128)}) %reduce-scatter.17.cloned.1.call-update) | async-done | bytes 221200 | tf_op jit(solution)/shard_map/reduce_scatter | solution.py:165
  645.4 33.5 %all_gather.25 = bf16[768,576]{0,1:T(8,128)(2,1)S(1)} all-gather(bf16[768,72]{0,1:T(8,128)(2,1)S(1)} %convert_element_type.185), channel_id=1, replica_groups=mesh['dp'=8,'tensor'=4] {'dp'}, dimensions={1}, use_global_device_ids=true | all-gather | bytes 995328 | tf_op jit(solution)/shard_map/all_gather | solution.py:175
  680.3 8.9 %all-gather.6.cloned.1.call-done = bf16[768,768]{0,1:T(8,128)(2,1)} async-done(((bf16[768,96]{0,1:T(8,128)(2,1)}), bf16[768,768]{0,1:T(8,128)(2,1)}) %all-gather.6.cloned.1.call-update) | async-done | bytes 1179664 | tf_op jit(solution)/shard_map/all_gather | solution.py:187
  691.9 39.8 %all-gather.8.cloned.1.call-done = bf16[768,768]{0,1:T(8,128)(2,1)} async-done(((bf16[768,96]{0,1:T(8,128)(2,1)}), bf16[768,768]{0,1:T(8,128)(2,1)}) %all-gather.8.cloned.1.call-update) | async-done | bytes 1179664 | tf_op jit(solution)/shard_map/all_gather | solution.py:193
  (212 shorter events, 92.9 us)
Async XLA Ops:
  7.2 53.4 %copy-start = (bf16[768,768]{1,0:T(8,128)(2,1)S(1)}, bf16[768,768]{1,0:T(8,128)(2,1)}, u32[]{:S(2)}) copy-start(bf16[768,768]{1,0:T(8,128)(2,1)} %param.25) | copy-start | bytes 3538948
  7.2 3.0 copy-start.24
  7.2 3.0 copy-start.22
  7.2 51.3 %all-reduce.7.cloned.1.call-start = ((), (), s32[]{:S(2)}) async-start(), calls=%async_computation.7 | async-start | bytes 1228800 | tf_op jit(solution)/shard_map/psum | solution.py:96
  21.9 78.9 %all-reduce.9.cloned.1.call-start = ((), (), s32[]{:S(2)}) async-start(), calls=%async_computation.8 | async-start | bytes 1228800 | tf_op jit(solution)/shard_map/psum | solution.py:117
  23.3 35.3 %copy-start.25 = (f32[768]{0:T(1024)S(1)}, f32[768]{0:T(1024)}, u32[]{:S(2)}) copy-start(f32[768]{0:T(1024)} %param.22) | copy-start | bytes 9220
  25.1 35.1 %copy-start.31 = (f32[2]{0:T(128)}, f32[2]{0:T(128)S(1)}, u32[]{:S(2)}) copy-start(f32[2]{0:T(128)S(1)} %compare_convert_fusion) | copy-start | bytes 28
  66.5 101.7 %all-reduce.11.cloned.1.call-start = ((), (), s32[]{:S(2)}) async-start(), calls=%async_computation.18 | async-start | bytes 2457600 | tf_op jit(solution)/shard_map/psum | solution.py:106
  107.8 4.5 copy-start.19
  129.6 112.1 %reduce-scatter.19.cloned.1.call-start = ((), (), s32[]{:S(2)}) async-start(), calls=%async_computation.10 | async-start | bytes 2654208 | tf_op jit(solution)/shard_map/reduce_scatter | solution.py:169
  133.7 172.5 %reduce-scatter.29.cloned.1.call-start = ((), (), s32[]{:S(2)}) async-start(), calls=%async_computation.17 | async-start | bytes 442368
  136.2 235.0 %reduce-scatter.27.cloned.1.call-start = ((), (), s32[]{:S(2)}) async-start(), calls=%async_computation.16 | async-start | bytes 442368
  137.2 306.7 %reduce-scatter.21.cloned.1.call-start = ((), (), s32[]{:S(2)}) async-start(), calls=%async_computation.12 | async-start | bytes 2654208 | tf_op jit(solution)/shard_map/reduce_scatter | solution.py:171
  140.9 367.6 %reduce-scatter.23.cloned.1.call-start = ((), (), s32[]{:S(2)}) async-start(), calls=%async_computation.14 | async-start | bytes 442368
  168.2 3.2 copy-start.14
  171.4 402.7 %reduce-scatter.25.cloned.1.call-start = ((), (), s32[]{:S(2)}) async-start(), calls=%async_computation.15 | async-start | bytes 884736
  176.2 468.3 %reduce-scatter.17.cloned.1.call-start = ((), (), s32[]{:S(2)}) async-start(), calls=%async_computation.9 | async-start | bytes 1990656 | tf_op jit(solution)/shard_map/reduce_scatter | solution.py:165
  180.3 63.2 %copy-start.28 = (u32[32]{0:T(128)S(1)}, u32[32]{0:T(128)}, u32[]{:S(2)}) copy-start(u32[32]{0:T(128)} %constant.41) | copy-start | bytes 388
  180.3 147.2 %copy-start.29 = (f32[3,64]{1,0:T(4,128)S(1)}, f32[3,64]{1,0:T(4,128)}, u32[]{:S(2)}) copy-start(f32[3,64]{1,0:T(4,128)} %get-tuple-element.107) | copy-start | bytes 2308
  180.3 266.0 %copy-start.26 = (f32[768]{0:T(1024)S(1)}, f32[768]{0:T(1024)}, u32[]{:S(2)}) copy-start(f32[768]{0:T(1024)} %param.28) | copy-start | bytes 9220
  180.3 508.8 %all-gather.6.cloned.1.call-start = ((), (), s32[]{:S(2)}) async-start(), calls=%async_computation.11 | async-start | bytes 1327104 | tf_op jit(solution)/shard_map/all_gather | solution.py:187
  243.4 488.2 %all-gather.8.cloned.1.call-start = ((), (), s32[]{:S(2)}) async-start(), calls=%async_computation.13 | async-start | bytes 1327104 | tf_op jit(solution)/shard_map/all_gather | solution.py:193
  446.3 6.7 copy-start.10
  448.5 4.6 copy-start.2
  (26 other events, 38.3 us)
Sparse Core Ops, SparseCore 0:
  22.0 36.4 all-reduce.6
  66.6 34.0 all-reduce.8
  129.7 38.4 all-reduce.10
  172.1 69.5 reduce-scatter.18
  244.8 61.3 reduce-scatter.28
  309.9 61.2 reduce-scatter.26
  375.3 68.6 reduce-scatter.20
  447.2 61.3 reduce-scatter.22
  511.9 62.2 reduce-scatter.24
  578.0 66.4 reduce-scatter.16
  646.7 42.4 all-gather.5
  691.2 40.3 all-gather.7
where the time goes:
time: 743 us; the launch traced here: 741 us
  waiting for transfers between devices  455 us (61%)
  blocking collectives  158 us (21%)
  local copies, waits for them, and re-layouts  47.1 us (6%)
  matrix products  41.1 us (6%)
  other arithmetic  22.2 us (3%)
  between operations  16.8 us (2%)
    unnamed x16, waiting for transfers between devices  166 us
    reduce_scatter x1, waiting for transfers between devices, per_device(): lax.psum_scatter(mlp_grads[0], 'dp', scatter_dimension=1, tiled=True)  61.4 us
    reduce_scatter x1, waiting for transfers between devices, per_device(): lax.psum_scatter(mlp_grads[2], 'dp', scatter_dimension=1, tiled=True)  52.8 us
    all_gather x1, waiting for transfers between devices, per_device(): lax.all_gather(shares[6].astype(jnp.bfloat16), 'dp', axis=1, tiled=True)  39.8 us
    unnamed x2, blocking collectives  36.6 us
    reduce_scatter x1, waiting for transfers between devices, per_device(): lax.psum_scatter(attn_grads[0], 'dp', scatter_dimension=1, tiled=True)  36.5 us
    all_gather x1, blocking collectives, per_device(): lax.all_gather(shares[0].astype(jnp.bfloat16), 'dp', axis=1, tiled=True)  33.5 us
    psum x1, waiting for transfers between devices, per_device(): lax.psum(attn_part.astype(jnp.bfloat16), 'tensor').astype(jnp.float32)  33.3 us
  transfers between devices with their start and end apart: 12, of which 12 were waited for; matrix products, arithmetic and copies ran while one was open for 7% of the time, Pallas kernels for 0%

commit v1 on v0

--- a/solution.py
+++ b/solution.py
@@ -190,9 +190,12 @@
         lax.all_gather(shares[5].astype(jnp.bfloat16), "dp", axis=1, tiled=True).astype(
             jnp.float32
         ),
-        lax.all_gather(shares[6].astype(jnp.bfloat16), "dp", axis=1, tiled=True).astype(
-            jnp.float32
-        ),
+        jnp.concatenate(
+            lax.all_to_all(
+                jnp.stack([shares[6].astype(jnp.bfloat16)] * lax.axis_size("dp")), "dp", 0, 0
+            ),
+            axis=1,
+        ).astype(jnp.float32),
         lax.all_gather(shares[7].astype(jnp.bfloat16), "dp", axis=1, tiled=True).astype(
             jnp.float32
         ),

time: 743 us -> 716 us (0.964)
  waiting for transfers between devices: 455 us -> 421 us
    all_gather x1 -> x0, waiting for transfers between devices: 39.8 us -> none  [per_device(): lax.all_gather(shares[6].astype(jnp.bfloat16), 'dp', axis=1, tiled=True)]
    reduce_scatter x1, waiting for transfers between devices: 61.4 us -> 82 us  [per_device(): lax.psum_scatter(mlp_grads[0], 'dp', scatter_dimension=1, tiled=True)]
    unnamed x16 -> x15, waiting for transfers between devices: 166 us -> 155 us
    unnamed x97 -> x99, local copies, waits for them, and re-layouts: 26.6 us -> 28 us
  transfers between devices with their start and end apart: 12 -> 12, of which waited for: 12 -> 11; matrix products, arithmetic and copies ran while one was open for 7% -> 8% of each run, Pallas kernels for 0% -> 0%
where the time goes in v1:
time: 716 us; the launch traced here: 714 us
  waiting for transfers between devices  421 us (59%)
  blocking collectives  158 us (22%)
  local copies, waits for them, and re-layouts  49.5 us (7%)
  matrix products  40.1 us (6%)
  other arithmetic  24.5 us (3%)
  between operations  16.4 us (2%)
    unnamed x15, waiting for transfers between devices  155 us
    reduce_scatter x1, waiting for transfers between devices, per_device(): lax.psum_scatter(mlp_grads[0], 'dp', scatter_dimension=1, tiled=True)  82 us
    reduce_scatter x1, waiting for transfers between devices, per_device(): lax.psum_scatter(mlp_grads[2], 'dp', scatter_dimension=1, tiled=True)  52.9 us
    unnamed x2, blocking collectives  36.7 us
    reduce_scatter x1, waiting for transfers between devices, per_device(): lax.psum_scatter(attn_grads[0], 'dp', scatter_dimension=1, tiled=True)  36.1 us
    all_gather x1, blocking collectives, per_device(): lax.all_gather(shares[0].astype(jnp.bfloat16), 'dp', axis=1, tiled=True)  33.5 us
    psum x1, waiting for transfers between devices, per_device(): lax.psum(attn_part.astype(jnp.bfloat16), 'tensor').astype(jnp.float32)  33.3 us
    all_gather x1, blocking collectives, per_device(): lax.all_gather(shares[2].astype(jnp.bfloat16), 'dp', axis=1, tiled=True)  31.8 us
  transfers between devices with their start and end apart: 12, of which 11 were waited for; matrix products, arithmetic and copies ran while one was open for 8% of the time, Pallas kernels for 0%

profile of v1, /device:TPU:0, one launch (start us, length us, event | category | flops | bytes accessed | tf_op | source)
XLA Modules:
  0.0 714.1 jit_solution(2763413078634612982)
XLA Ops:
  25.3 33.3 %all-reduce.7.cloned.1.call-done = bf16[394,768]{1,0:T(8,128)(2,1)} async-done(((bf16[394,768]{1,0:T(8,128)(2,1)}), bf16[394,768]{1,0:T(8,128)(2,1)}) %all-reduce.7.cloned.1.call-update) | async-done | bytes 605200 | tf_op jit(solution)/shard_map/psum | solution.py:96
  69.7 31.0 %all-reduce.9.cloned.1.call-done = bf16[394,768]{1,0:T(8,128)(2,1)} async-done(((bf16[394,768]{1,0:T(8,128)(2,1)}), bf16[394,768]{1,0:T(8,128)(2,1)}) %all-reduce.9.cloned.1.call-update) | async-done | bytes 605200 | tf_op jit(solution)/shard_map/psum | solution.py:117
  107.8 4.5 fusion.69
  112.2 3.8 fusion.34
  133.1 3.6 convolution_multiply_fusion
  141.3 26.9 %all-reduce.11.cloned.1.call-done = (bf16[394,768]{1,0:T(8,128)(2,1)}, bf16[394,768]{1,0:T(8,128)(2,1)}) async-done(((bf16[394,768]{1,0:T(8,128)(2,1)}, bf16[394,768]{1,0:T(8,128)(2,1)}), (bf16[394,768]{1,0:T(8,128)(2,1)}, bf16[394,768]{1,0:T(8,128)(2,1)})) %all-reduce.11.cloned.1.call-update) | async-done | bytes 1210384 | tf_op jit(solution)/shard_map/psum | solution.py:106
  177.1 3.1 convolution_multiply_fusion.2
  182.7 50.7 %reduce-scatter.29.cloned.1.call-done = f32[96,1]{1,0:T(8,128)} async-done(((f32[768,1]{1,0:T(8,128)}), f32[96,1]{1,0:T(8,128)}) %reduce-scatter.29.cloned.1.call-update) | async-done | bytes 400
  234.5 19.6 %all-reduce = bf16[768]{0:T(1024)(128)(2,1)S(1)} all-reduce(bf16[768]{0:T(1024)(128)(2,1)S(1)} %dynamic-update-slice), channel_id=1, replica_groups=mesh['dp'=8,'tensor'=4] {'dp'}, use_global_device_ids=true, to_apply=%add | all-reduce | flops 768 | bytes 3072
  254.9 17.1 %all-reduce.1 = bf16[2,192]{1,0:T(2,128)(2,1)S(1)} all-reduce(f32[2,192]{1,0:T(2,128)S(1)} %maximum_multiply_fusion.2), channel_id=4, replica_groups=mesh['dp'=8,'tensor'=4] {'dp'}, use_global_device_ids=true, to_apply=%region_22.0.clone | all-reduce | flops 384 | bytes 2304
  272.1 18.3 %all-gather.1 = bf16[8,24,2]{1,2,0:T(2,128)(2,1)S(1)} all-gather(bf16[1,24,2]{1,2,0:T(2,128)(2,1)S(1)} %fusion.60), channel_id=1, replica_groups=mesh['dp'=8,'tensor'=4] {'dp'}, dimensions={0}, use_global_device_ids=true | all-gather | bytes 864 | tf_op jit(solution)/shard_map/all_gather | solution.py:178
  291.1 7.3 %reduce-scatter.27.cloned.1.call-done = f32[96,3]{1,0:T(8,128)} async-done(((f32[768,3]{1,0:T(8,128)}), f32[96,3]{1,0:T(8,128)}) %reduce-scatter.27.cloned.1.call-update) | async-done | bytes 1168
  299.3 18.8 %all-gather.2 = bf16[8,96,3]{1,2,0:T(4,128)(2,1)S(1)} all-gather(bf16[1,96,3]{1,2,0:T(4,128)(2,1)S(1)} %bitcast.111), channel_id=1, replica_groups=mesh['dp'=8,'tensor'=4] {'dp'}, dimensions={0}, use_global_device_ids=true | all-gather | bytes 5184 | tf_op jit(solution)/shard_map/all_gather | solution.py:199
  318.1 52.9 %reduce-scatter.21.cloned.1.call-done = f32[768,96]{0,1:T(8,128)} async-done(((f32[768,768]{0,1:T(8,128)}), f32[768,96]{0,1:T(8,128)}) %reduce-scatter.21.cloned.1.call-update) | async-done | bytes 294928 | tf_op jit(solution)/shard_map/reduce_scatter | solution.py:171
  373.1 4.4 all-to-all-start
  377.7 82.0 %reduce-scatter.19.cloned.1.call-done = f32[768,96]{0,1:T(8,128)} async-done(((f32[768,768]{0,1:T(8,128)}), f32[768,96]{0,1:T(8,128)}) %reduce-scatter.19.cloned.1.call-update) | async-done | bytes 294928 | tf_op jit(solution)/shard_map/reduce_scatter | solution.py:169
  472.7 51.7 %reduce-scatter.23.cloned.1.call-done = f32[96,3]{1,0:T(8,128)} async-done(((f32[768,3]{1,0:T(8,128)}), f32[96,3]{1,0:T(8,128)}) %reduce-scatter.23.cloned.1.call-update) | async-done | bytes 1168
  525.2 18.7 %all-gather = bf16[8,96,3]{1,2,0:T(4,128)(2,1)S(1)} all-gather(bf16[1,96,3]{1,2,0:T(4,128)(2,1)S(1)} %bitcast.112), channel_id=1, replica_groups=mesh['dp'=8,'tensor'=4] {'dp'}, dimensions={0}, use_global_device_ids=true | all-gather | bytes 5184 | tf_op jit(solution)/shard_map/all_gather | solution.py:184
  544.6 45.4 %reduce-scatter.25.cloned.1.call-done = f32[96,192]{1,0:T(8,128)} async-done(((f32[768,192]{1,0:T(8,128)}), f32[96,192]{1,0:T(8,128)}) %reduce-scatter.25.cloned.1.call-update) | async-done | bytes 73744
  591.0 31.8 %all_gather.24 = bf16[192,768]{0,1:T(8,128)(2,1)S(1)} all-gather(bf16[192,96]{0,1:T(8,128)(2,1)S(1)} %copy.157), channel_id=1, replica_groups=mesh['dp'=8,'tensor'=4] {'dp'}, dimensions={1}, use_global_device_ids=true | all-gather | bytes 331776 | tf_op jit(solution)/shard_map/all_gather | solution.py:181
  623.8 36.1 %reduce-scatter.17.cloned.1.call-done = f32[768,72]{0,1:T(8,128)} async-done(((f32[768,576]{0,1:T(8,128)}), f32[768,72]{0,1:T(8,128)}) %reduce-scatter.17.cloned.1.call-update) | async-done | bytes 221200 | tf_op jit(solution)/shard_map/reduce_scatter | solution.py:165
  660.9 33.5 %all_gather.22 = bf16[768,576]{0,1:T(8,128)(2,1)S(1)} all-gather(bf16[768,72]{0,1:T(8,128)(2,1)S(1)} %convert_element_type.191), channel_id=1, replica_groups=mesh['dp'=8,'tensor'=4] {'dp'}, dimensions={1}, use_global_device_ids=true | all-gather | bytes 995328 | tf_op jit(solution)/shard_map/all_gather | solution.py:175
  698.6 3.0 copy.163
  701.6 3.2 all-gather.5.cloned.1.call-done
  (215 shorter events, 97.1 us)
Async XLA Ops:
  7.2 53.4 %copy-start = (bf16[768,768]{1,0:T(8,128)(2,1)S(1)}, bf16[768,768]{1,0:T(8,128)(2,1)}, u32[]{:S(2)}) copy-start(bf16[768,768]{1,0:T(8,128)(2,1)} %param.25) | copy-start | bytes 3538948
  7.2 3.0 copy-start.24
  7.2 3.0 copy-start.22
  7.2 51.3 %all-reduce.7.cloned.1.call-start = ((), (), s32[]{:S(2)}) async-start(), calls=%async_computation.8 | async-start | bytes 1228800 | tf_op jit(solution)/shard_map/psum | solution.py:96
  11.6 2.6 copy-start.8
  21.9 78.8 %all-reduce.9.cloned.1.call-start = ((), (), s32[]{:S(2)}) async-start(), calls=%async_computation.9 | async-start | bytes 1228800 | tf_op jit(solution)/shard_map/psum | solution.py:117
  23.3 35.3 %copy-start.25 = (f32[768]{0:T(1024)S(1)}, f32[768]{0:T(1024)}, u32[]{:S(2)}) copy-start(f32[768]{0:T(1024)} %param.22) | copy-start | bytes 9220
  25.1 35.1 %copy-start.31 = (f32[2]{0:T(128)}, f32[2]{0:T(128)S(1)}, u32[]{:S(2)}) copy-start(f32[2]{0:T(128)S(1)} %compare_convert_fusion) | copy-start | bytes 28
  66.5 101.6 %all-reduce.11.cloned.1.call-start = ((), (), s32[]{:S(2)}) async-start(), calls=%async_computation.18 | async-start | bytes 2457600 | tf_op jit(solution)/shard_map/psum | solution.py:106
  107.8 4.5 copy-start.19
  129.5 103.9 %reduce-scatter.29.cloned.1.call-start = ((), (), s32[]{:S(2)}) async-start(), calls=%async_computation.17 | async-start | bytes 442368
  132.0 166.4 %reduce-scatter.27.cloned.1.call-start = ((), (), s32[]{:S(2)}) async-start(), calls=%async_computation.16 | async-start | bytes 442368
  133.0 238.0 %reduce-scatter.21.cloned.1.call-start = ((), (), s32[]{:S(2)}) async-start(), calls=%async_computation.13 | async-start | bytes 2654208 | tf_op jit(solution)/shard_map/reduce_scatter | solution.py:171
  136.7 323.0 %reduce-scatter.19.cloned.1.call-start = ((), (), s32[]{:S(2)}) async-start(), calls=%async_computation.11 | async-start | bytes 2654208 | tf_op jit(solution)/shard_map/reduce_scatter | solution.py:169
  140.2 384.2 %reduce-scatter.23.cloned.1.call-start = ((), (), s32[]{:S(2)}) async-start(), calls=%async_computation.14 | async-start | bytes 442368
  168.1 3.2 copy-start.14
  171.3 418.6 %reduce-scatter.25.cloned.1.call-start = ((), (), s32[]{:S(2)}) async-start(), calls=%async_computation.15 | async-start | bytes 884736
  176.1 483.8 %reduce-scatter.17.cloned.1.call-start = ((), (), s32[]{:S(2)}) async-start(), calls=%async_computation.10 | async-start | bytes 1990656 | tf_op jit(solution)/shard_map/reduce_scatter | solution.py:165
  180.2 74.6 %copy-start.29 = (f32[3,64]{1,0:T(4,128)S(1)}, f32[3,64]{1,0:T(4,128)}, u32[]{:S(2)}) copy-start(f32[3,64]{1,0:T(4,128)} %get-tuple-element.107) | copy-start | bytes 2308
  373.1 89.0 %copy-start.26 = (f32[768]{0:T(1024)S(1)}, f32[768]{0:T(1024)}, u32[]{:S(2)}) copy-start(f32[768]{0:T(1024)} %param.28) | copy-start | bytes 9220
  373.1 322.6 %all-to-all-start = ((bf16[8,768,96]{1,2,0:T(8,128)(2,1)}), bf16[8,768,96]{1,2,0:T(8,128)(2,1)}, u32[]{:S(2)}, u32[]{:S(2)}) async-start(bf16[8,768,96]{1,2,0:T(8,128)(2,1)} %stack.64), calls=%async_computation.3 | async-start | bytes 2359296 | tf_op jit(solution)/shard_map/all_to_all | solution.py:194
  377.5 327.4 %all-gather.5.cloned.1.call-start = ((), (), s32[]{:S(2)}) async-start(), calls=%async_computation.12 | async-start | bytes 1327104 | tf_op jit(solution)/shard_map/all_gather | solution.py:187
  462.1 6.8 copy-start.10
  464.3 4.6 copy-start.2
  (27 other events, 37.5 us)
Sparse Core Ops, SparseCore 0:
  22.0 36.4 all-reduce.6
  66.6 34.0 all-reduce.8
  129.6 38.4 all-reduce.10
  171.2 62.1 reduce-scatter.28
  237.1 61.2 reduce-scatter.26
  302.3 68.6 reduce-scatter.20
  375.1 84.6 reduce-scatter.18
  463.0 61.2 reduce-scatter.22
  527.6 62.2 reduce-scatter.24
  593.8 66.0 reduce-scatter.16
  662.1 42.6 all-gather.4
